TPU v7x, 32 devices: a whole 2x2x4 slice. The times are simulated.
32 devices in a mesh: item: 4 (over y, x), user: 4 (over z), edge: 2 (over core).
Axes of the slice: x: 2, y: 2, z: 4, core: 2. Of those that a mesh axis runs over, the one named last changes fastest.
Arguments:
- item_emb: bfloat16 [16384, 256], P('item'), may hold values from -6 to 6
- user_emb: bfloat16 [24576, 256], P('user'), may hold values from -6 to 6
- block_item: int32 [4, 4, 2, 96], P('item', 'user', 'edge'), may hold values from 0 to 31
- block_user: int32 [4, 4, 2, 96], P('item', 'user', 'edge'), may hold values from 0 to 47
- block_rows: int32 [4, 4, 2, 96, 128], P('item', 'user', 'edge'), may hold values from 0 to 127
- block_count: int32 [4, 4, 2], P('item', 'user', 'edge'), may hold values from 1 to 96, as said below
- user_weight: bfloat16 [256, 256], replicated, may hold values from -3.5 to 3.5
- up_weight: bfloat16 [256, 1024], replicated, may hold values from -0.375 to 0.375
- down_weight: bfloat16 [1024, 256], replicated, may hold values from -0.1875 to 0.1875
Outputs:
- new_items: bfloat16 [16384, 256], P(('item', 'user', 'edge'))
Inputs may be any that keep to these rules, and one draw needn't show every extreme that they name: `block_count`: some list has exactly 96 live slots in every draw; entries of slots that are not live are ignored.
All inputs are finite; a program needn't handle non-finite values.
Results may differ from a plain program's by a relative error of at most 0.0045.
Values may be sent and summed in bfloat16 or wider, within the bound.
No kernel may reach another device: no remote copies, remote signals or barrier semaphores. Data moves between devices by JAX's collectives and lax.ppermute only.
A program may use at most 64 MiB of HBM per device.

v0:
```python
import jax
import jax.numpy as jnp
from jax import lax
from jax.sharding import PartitionSpec as P

TILE = 128


def refresh(summed, degree, own_rows, user_weight):
    average = (summed / jnp.maximum(degree, 1.0)[:, None]).astype(jnp.bfloat16)
    projected = jnp.dot(average, user_weight, preferred_element_type=jnp.float32)
    return (own_rows.astype(jnp.float32) + jax.nn.silu(projected)).astype(jnp.bfloat16)


def body(
    item_emb,
    user_emb,
    block_item,
    block_user,
    block_rows,
    block_count,
    user_weight,
    up_weight,
    down_weight,
):
    channels = item_emb.shape[1]
    item_tiles = item_emb.shape[0] // TILE
    user_tiles = user_emb.shape[0] // TILE
    slot_items = block_item.reshape(-1)
    slot_users = block_user.reshape(-1)
    slot_links = block_rows.reshape(-1, TILE)
    live_count = block_count.reshape(())
    slots = slot_items.shape[0]
    per_turn = min(32, slots)
    rounds = (live_count + per_turn - 1) // per_turn
    inside = jnp.arange(TILE, dtype=jnp.int32)
    tiled_items = item_emb.reshape(item_tiles, TILE, channels)

    def pieces(which):
        offset = which * per_turn
        items_at = lax.dynamic_slice_in_dim(slot_items, offset, per_turn, 0)
        users_at = lax.dynamic_slice_in_dim(slot_users, offset, per_turn, 0)
        links = lax.dynamic_slice_in_dim(slot_links, offset, per_turn, 0)
        alive = offset + jnp.arange(per_turn, dtype=jnp.int32) < live_count
        onehot = ((links[:, :, None] == inside[None, None, :]) & alive[:, None, None]).astype(
            jnp.bfloat16
        )
        return (items_at, users_at, onehot, alive)

    def first_hop(which, carry):
        summed, degree = carry
        items_at, users_at, onehot, alive = pieces(which)
        gathered = jnp.take(tiled_items, items_at, axis=0)
        contrib = jnp.einsum("grc,grd->gcd", onehot, gathered, preferred_element_type=jnp.float32)
        chooser = (jnp.arange(user_tiles, dtype=jnp.int32)[:, None] == users_at[None, :]).astype(
            jnp.float32
        )
        summed = summed + jnp.einsum(
            "sg,gcd->scd", chooser, contrib, precision=lax.Precision.HIGHEST
        )
        column_hits = jnp.sum(onehot.astype(jnp.float32), axis=1)
        degree = degree + jnp.dot(chooser, column_hits, precision=lax.Precision.HIGHEST)
        return (summed, degree)

    start = (
        jnp.zeros((user_tiles, TILE, channels), jnp.float32),
        jnp.zeros((user_tiles, TILE), jnp.float32),
    )
    user_part, user_hits = lax.fori_loop(0, rounds, first_hop, start)
    user_part = user_part.reshape(-1, channels)
    user_hits = user_hits.reshape(-1)
    share_sum, share_hits = (
        lax.psum_scatter(user_part, ("item", "edge"), scatter_dimension=0, tiled=True),
        lax.psum_scatter(user_hits, ("item", "edge"), scatter_dimension=0, tiled=True),
    )
    share_rows = share_sum.shape[0]
    position = lax.axis_index("item") * lax.axis_size("edge") + lax.axis_index("edge")
    own_rows = lax.dynamic_slice_in_dim(user_emb, position * share_rows, share_rows, 0)
    mine = refresh(share_sum, share_hits, own_rows, user_weight)
    user_new = lax.all_gather(mine, ("item", "edge"), axis=0, tiled=True)
    tiled_users = user_new.reshape(user_tiles, TILE, channels)

    def second_hop(which, carry):
        summed, degree = carry
        items_at, users_at, onehot, alive = pieces(which)
        gathered = jnp.take(tiled_users, users_at, axis=0)
        contrib = jnp.einsum("grc,gcd->grd", onehot, gathered, preferred_element_type=jnp.float32)
        chooser = (
            (jnp.arange(item_tiles, dtype=jnp.int32)[:, None] == items_at[None, :]) & alive[None, :]
        ).astype(jnp.float32)
        summed = summed + jnp.einsum(
            "sg,grd->srd", chooser, contrib, precision=lax.Precision.HIGHEST
        )
        degree = degree + jnp.sum(chooser, axis=1)
        return (summed, degree)

    start = (
        jnp.zeros((item_tiles, TILE, channels), jnp.float32),
        jnp.zeros((item_tiles,), jnp.float32),
    )
    item_part, tile_hits = lax.fori_loop(0, rounds, second_hop, start)
    item_part = item_part.reshape(-1, channels)
    item_hits = jnp.broadcast_to(tile_hits[:, None], (item_tiles, TILE)).reshape(-1)
    edge_count = lax.axis_size("edge")
    item_sum, item_degree = (
        lax.psum_scatter(item_part, ("user", "edge"), scatter_dimension=0, tiled=True),
        lax.psum_scatter(item_hits, ("user", "edge"), scatter_dimension=0, tiled=True),
    )
    share_rows = item_sum.shape[0]
    position = lax.axis_index("user") * edge_count + lax.axis_index("edge")
    own_items = lax.dynamic_slice_in_dim(item_emb, position * share_rows, share_rows, 0)
    merged = own_items.astype(jnp.float32) + item_sum / jnp.maximum(item_degree, 1.0)[:, None]
    hidden = jax.nn.silu(
        jnp.dot(merged.astype(jnp.bfloat16), up_weight, preferred_element_type=jnp.float32)
    ).astype(jnp.bfloat16)
    return (merged + jnp.dot(hidden, down_weight, preferred_element_type=jnp.float32)).astype(
        jnp.bfloat16
    )


def solution(mesh):
    return jax.shard_map(
        body,
        mesh=mesh,
        in_specs=(
            P("item", None),
            P("user", None),
            P("item", "user", "edge", None),
            P("item", "user", "edge", None),
            P("item", "user", "edge", None, None),
            P("item", "user", "edge"),
            P(),
            P(),
            P(),
        ),
        out_specs=P(("item", "user", "edge"), None),
        check_vma=False,
    )
```

profile of v0, /device:TPU:0, one launch (start us, length us, event | category | flops | bytes accessed | tf_op | source)
XLA Modules:
  0.0 276.3 jit_solution(5834216098491183925)
XLA Ops:
  7.3 3.4 %broadcast_in_dim.57 = f32[48,128,256]{2,0,1:T(8,128)} broadcast(f32[]{:T(128)} %constant.94.clone.1), dimensions={} | broadcast | bytes 6291460 | tf_op jit(solution)/shard_map/broadcast_in_dim | solution.py:66
  10.7 48.7 %while.26 = (s32[]{:T(128)}, f32[48,128,256]{2,0,1:T(8,128)}, f32[48,128]{1,0:T(8,128)S(1)}, s32[]{:T(128)}, s32[96]{0:T(128)S(1)}, /*index=5*/s32[96,128]{1,0:T...) while((s32[]{:T(128)}, f32[48,128,256]{2,0,1:T(8,128)}, ...), condition=%wide.region_2.3_spmd.clone, body=%wide.region_0.2_spmd.clone.sunk | while | flops 881072384 | bytes 77747608 | solution.py:69
  16.6 6.5 %fusion.77 = f32[48,128,256]{2,0,1:T(8,128)S(1)} fusion(f32[48,128,256]{2,0,1:T(8,128)S(1)} %copy-done.1, f32[32,128,256]{2,1,0:T(8,128)S(1)} %fusion.76, s32[32]{0:T(128)S(1)} %dynamic_slice.49), kind=kOutput, calls=%fused_computation.6.clone.1 | convolution fusion | flops 605554176 | bytes 16777344 | tf_op jit(solution)/shard_map/while/body/sg,gcd->scd/dot_general | solution.py:58
  23.1 2.6 copy-done.2
  32.8 6.5 %fusion.77 = f32[48,128,256]{2,0,1:T(8,128)S(1)} fusion(f32[48,128,256]{2,0,1:T(8,128)S(1)} %copy-done.1, f32[32,128,256]{2,1,0:T(8,128)S(1)} %fusion.76, s32[32]{0:T(128)S(1)} %dynamic_slice.49), kind=kOutput, calls=%fused_computation.6.clone.1 | convolution fusion | flops 605554176 | bytes 16777344 | tf_op jit(solution)/shard_map/while/body/sg,gcd->scd/dot_general | solution.py:58
  39.3 2.6 copy-done.2
  48.9 6.5 %fusion.77 = f32[48,128,256]{2,0,1:T(8,128)S(1)} fusion(f32[48,128,256]{2,0,1:T(8,128)S(1)} %copy-done.1, f32[32,128,256]{2,1,0:T(8,128)S(1)} %fusion.76, s32[32]{0:T(128)S(1)} %dynamic_slice.49), kind=kOutput, calls=%fused_computation.6.clone.1 | convolution fusion | flops 605554176 | bytes 16777344 | tf_op jit(solution)/shard_map/while/body/sg,gcd->scd/dot_general | solution.py:58
  55.5 2.6 copy-done.2
  59.5 9.1 %copy.15 = f32[48,128,256]{2,1,0:T(8,128)} copy(f32[48,128,256]{2,0,1:T(8,128)} %get-tuple-element.113) | data formatting | bytes 12582912 | tf_op jit(solution)/shard_map/while | solution.py:69
  70.4 25.5 %all-reduce = f32[6144]{0:T(1024)S(1)} all-reduce(f32[6144]{0:T(1024)S(1)} %bitcast.35), channel_id=3, replica_groups=mesh['item'=4,'user'=4,'edge'=2] {'item','edge'}, use_global_device_ids=true, to_apply=%region_4.5.clone | all-reduce | flops 6144 | bytes 49152
  96.1 36.6 %reduce-scatter.3.cloned.1.call-done = f32[768,256]{1,0:T(8,128)} async-done(((f32[6144,256]{1,0:T(8,128)}), f32[768,256]{1,0:T(8,128)}) %reduce-scatter.3.cloned.1.call-update) | async-done | bytes 786448 | tf_op jit(solution)/shard_map/reduce_scatter | solution.py:73
  135.2 32.3 %all-gather.2.cloned.1.call-done = bf16[6144,256]{1,0:T(8,128)(2,1)} async-done(((bf16[768,256]{1,0:T(8,128)(2,1)}), bf16[6144,256]{1,0:T(8,128)(2,1)}) %all-gather.2.cloned.1.call-update) | async-done | bytes 3145744 | tf_op jit(solution)/shard_map/all_gather | solution.py:80
  167.5 2.5 broadcast_in_dim.55
  170.0 39.7 %while.27 = (s32[]{:T(128)}, f32[32,128,256]{2,0,1:T(8,128)}, f32[32]{0:T(128)S(1)}, s32[]{:T(128)}, s32[96]{0:T(128)S(1)}, /*index=5*/s32[]{:T(128)}, s32[96,12...) while((s32[]{:T(128)}, f32[32,128,256]{2,0,1:T(8,128)}, ...), condition=%wide.region_7.8_spmd.clone, body=%wide.region_5.7_spmd.clone.sunk | while | flops 674241792 | bytes 56678324 | solution.py:101
  170.7 2.6 gather_fusion.1
  175.9 5.1 %fusion.83 = f32[32,128,256]{2,0,1:T(8,128)S(1)} fusion(f32[32,128,256]{2,0,1:T(8,128)S(1)} %copy-done.3, f32[32,128,256]{2,1,0:T(8,128)S(1)} %fusion.82, s32[32]{0:T(128)S(1)} %dynamic_slice.51, pred[32]{0:T(512)(128)(4,1)S(1)} %get-tuple-element.324), kind=kOutput, calls=%fused_computation.30.clone.1 | convolution fusion | flops 403703808 | bytes 12583072 | tf_op jit(solution)/shard_map/while/body/sg,grd->srd/dot_general | solution.py:91
  183.9 2.6 gather_fusion.1
  189.1 5.1 %fusion.83 = f32[32,128,256]{2,0,1:T(8,128)S(1)} fusion(f32[32,128,256]{2,0,1:T(8,128)S(1)} %copy-done.3, f32[32,128,256]{2,1,0:T(8,128)S(1)} %fusion.82, s32[32]{0:T(128)S(1)} %dynamic_slice.51, pred[32]{0:T(512)(128)(4,1)S(1)} %get-tuple-element.324), kind=kOutput, calls=%fused_computation.30.clone.1 | convolution fusion | flops 403703808 | bytes 12583072 | tf_op jit(solution)/shard_map/while/body/sg,grd->srd/dot_general | solution.py:91
  197.1 2.6 gather_fusion.1
  202.3 5.1 %fusion.83 = f32[32,128,256]{2,0,1:T(8,128)S(1)} fusion(f32[32,128,256]{2,0,1:T(8,128)S(1)} %copy-done.3, f32[32,128,256]{2,1,0:T(8,128)S(1)} %fusion.82, s32[32]{0:T(128)S(1)} %dynamic_slice.51, pred[32]{0:T(512)(128)(4,1)S(1)} %get-tuple-element.324), kind=kOutput, calls=%fused_computation.30.clone.1 | convolution fusion | flops 403703808 | bytes 12583072 | tf_op jit(solution)/shard_map/while/body/sg,grd->srd/dot_general | solution.py:91
  209.7 6.6 %copy.16 = f32[32,128,256]{2,1,0:T(8,128)} copy(f32[32,128,256]{2,0,1:T(8,128)} %get-tuple-element.115) | data formatting | bytes 8388608 | tf_op jit(solution)/shard_map/while | solution.py:101
  218.2 27.4 %all-reduce.1 = f32[4096]{0:T(1024)S(1)} all-reduce(f32[4096]{0:T(1024)S(1)} %broadcast_bitcast_fusion), channel_id=5, replica_groups=mesh['item'=4,'user'=4,'edge'=2] {'user','edge'}, use_global_device_ids=true, to_apply=%region_9.10.clone | all-reduce | flops 4096 | bytes 32768
  245.7 21.1 %reduce-scatter.5.cloned.1.call-done = f32[512,256]{1,0:T(8,128)} async-done(((f32[4096,256]{1,0:T(8,128)}), f32[512,256]{1,0:T(8,128)}) %reduce-scatter.5.cloned.1.call-update) | async-done | bytes 524304 | tf_op jit(solution)/shard_map/reduce_scatter | solution.py:106
  266.8 2.9 %fusion.42 = bf16[512,256]{1,0:T(8,128)(2,1)} fusion(bf16[1024,256]{1,0:T(8,128)(2,1)S(1)} %copy-done, bf16[256,1024]{1,0:T(8,128)(2,1)S(1)} %copy-done.8, f32[512,256]{1,0:T(8,128)} %reduce-scatter.5.cloned.1.call-done, f32[512]{0:T(512)S(1)} %dynamic-slice_maximum_fusion.1, bf16[4096,256]{1,0:T(8,128)(2,1)} %bitcast.31, s32[]{:T(128)S(6)} %select_n.38), kind=kOutput, calls=%fused_computation.53 | convolution fusion | flops 540672000 | bytes 2888704 | tf_op jit(solution)/shard_map/dot_general | solution.py:116
  (96 shorter events, 42.2 us)
Async XLA Ops:
  6.5 260.3 %copy-start = (bf16[1024,256]{1,0:T(8,128)(2,1)S(1)}, bf16[1024,256]{1,0:T(8,128)(2,1)}, u32[]{:S(2)}) copy-start(bf16[1024,256]{1,0:T(8,128)(2,1)} %param.21) | copy-start | bytes 1572868
  6.5 126.1 %reduce-scatter.3.cloned.1.call-start = ((), (), s32[]{:S(2)}) async-start(), calls=%async_computation.2 | async-start | bytes 7077888 | tf_op jit(solution)/shard_map/reduce_scatter | solution.py:73
  7.3 3.5 %copy-start.5 = (s32[1,1,1,96,128]{4,3,2,1,0:T(8,128)S(1)}, s32[1,1,1,96,128]{4,3,2,1,0:T(8,128)}, u32[]{:S(2)}) copy-start(s32[1,1,1,96,128]{4,3,2,1,0:T(8,128)} %param.17) | copy-start | bytes 147460
  7.3 3.5 %copy-start.6 = (s32[1,1,1,96]{3,2,1,0:T(1,128)S(1)}, s32[1,1,1,96]{3,2,1,0:T(1,128)}, u32[]{:S(2)}) copy-start(s32[1,1,1,96]{3,2,1,0:T(1,128)} %param.16) | copy-start | bytes 1156
  7.3 3.4 %copy-start.7 = (s32[1,1,1,96]{3,2,1,0:T(1,128)S(1)}, s32[1,1,1,96]{3,2,1,0:T(1,128)}, u32[]{:S(2)}) copy-start(s32[1,1,1,96]{3,2,1,0:T(1,128)} %param.15) | copy-start | bytes 1156
  13.8 2.8 %copy-start.1 = (f32[48,128,256]{2,0,1:T(8,128)S(1)}, f32[48,128,256]{2,0,1:T(8,128)}, u32[]{:S(2)}) copy-start(f32[48,128,256]{2,0,1:T(8,128)} %get-tuple-element.339) | copy-start | bytes 18874372 | tf_op jit(solution)/shard_map/while
  23.1 2.6 copy-start.2
  30.0 2.8 %copy-start.1 = (f32[48,128,256]{2,0,1:T(8,128)S(1)}, f32[48,128,256]{2,0,1:T(8,128)}, u32[]{:S(2)}) copy-start(f32[48,128,256]{2,0,1:T(8,128)} %get-tuple-element.339) | copy-start | bytes 18874372 | tf_op jit(solution)/shard_map/while
  39.3 2.6 copy-start.2
  46.2 2.8 %copy-start.1 = (f32[48,128,256]{2,0,1:T(8,128)S(1)}, f32[48,128,256]{2,0,1:T(8,128)}, u32[]{:S(2)}) copy-start(f32[48,128,256]{2,0,1:T(8,128)} %get-tuple-element.339) | copy-start | bytes 18874372 | tf_op jit(solution)/shard_map/while
  55.5 2.6 copy-start.2
  68.6 0.7 copy-start.11
  68.6 64.1 %copy-start.9 = (bf16[256,256]{1,0:T(8,128)(2,1)S(1)}, bf16[256,256]{1,0:T(8,128)(2,1)}, u32[]{:S(2)}) copy-start(bf16[256,256]{1,0:T(8,128)(2,1)} %param.19) | copy-start | bytes 393220
  68.6 98.9 %all-gather.2.cloned.1.call-start = ((), (), s32[]{:S(2)}) async-start(), calls=%async_computation.3 | async-start | bytes 3538944 | tf_op jit(solution)/shard_map/all_gather | solution.py:80
  135.1 131.7 %reduce-scatter.5.cloned.1.call-start = ((), (), s32[]{:S(2)}) async-start(), calls=%async_computation.4 | async-start | bytes 4718592 | tf_op jit(solution)/shard_map/reduce_scatter | solution.py:106
  173.3 2.6 copy-start.3
  181.0 2.0 copy-start.4
  186.5 2.6 copy-start.3
  194.2 2.0 copy-start.4
  199.7 2.6 copy-start.3
  207.4 2.0 copy-start.4
  216.3 0.7 copy-start.10
  216.3 50.5 %copy-start.8 = (bf16[256,1024]{1,0:T(8,128)(2,1)S(1)}, bf16[256,1024]{1,0:T(8,128)(2,1)}, u32[]{:S(2)}) copy-start(bf16[256,1024]{1,0:T(8,128)(2,1)} %param.20) | copy-start | bytes 1572868
Sparse Core Ops, SparseCore 0:
  68.7 63.9 reduce-scatter.2
  135.2 32.1 all-gather.1
  216.4 50.3 reduce-scatter.4
where the time goes:
time: 276 us
  waiting for transfers between devices  90 us (33%)
  local copies, waits for them, and re-layouts  58.7 us (21%)
  blocking collectives  53 us (19%)
  matrix products  51 us (18%)
  between operations  15.2 us (6%)
  other arithmetic  7.5 us (3%)
    unnamed x2, blocking collectives  53 us
    reduce_scatter x1, waiting for transfers between devices, body(): lax.psum_scatter(user_part, ('item', 'edge'), scatter_dimension=0, tiled=...  36.6 us
    all_gather x1, waiting for transfers between devices, body(): user_new = lax.all_gather(mine, ('item', 'edge'), axis=0, tiled=True)  32.3 us
    reduce_scatter x1, waiting for transfers between devices, body(): lax.psum_scatter(item_part, ('user', 'edge'), scatter_dimension=0, tiled=...  21.1 us
    dot_general x3, matrix products, first_hop(): jnp.einsum('sg,gcd->scd', chooser, contrib, precision=lax.Precision.HIGHEST)  19.6 us
    while x24, local copies, waits for them, and re-layouts  19.6 us
    dot_general x3, matrix products, second_hop(): jnp.einsum('sg,grd->srd', chooser, contrib, precision=lax.Precision.HIGHEST)  15.4 us
    while x1, local copies, waits for them, and re-layouts, body(): user_part, user_hits = lax.fori_loop(0, rounds, first_hop, start)  9.08 us
  transfers between devices with their start and end apart: 3, of which 3 were waited for; matrix products, arithmetic and copies ran while one was open for 1% of the time, Pallas kernels for 0%

commit v1 on v0

v1 whole, which is shorter than its diff:
```python
import functools

import jax
import jax.numpy as jnp
from jax import lax
from jax.experimental import pallas as pl
from jax.experimental.pallas import tpu as pltpu
from jax.sharding import PartitionSpec as P

TILE = 128
GROUP = 8
F32 = jnp.float32
BF16 = jnp.bfloat16
ANY = pl.BlockSpec(memory_space=pl.ANY)
VMEM = pl.BlockSpec(memory_space=pltpu.VMEM)
SMEM = pl.BlockSpec(memory_space=pltpu.SMEM)


def silu(v):
    return v / (1.0 + jnp.exp(-v))


def choose_slots(lists, slots, pick, slot_of, source_of, target_of):
    found = jnp.int32(0)
    for number, (items, users, count) in enumerate(lists):
        live = count[0]

        def step(b, found, number=number, items=items, users=users, live=live):
            source, target, mine = pick(items[b], users[b])
            slot_of[found] = number * slots + b
            source_of[found] = source
            target_of[found] = target
            return found + jnp.where(jnp.logical_and(mine, b < live), 1, 0)

        found = lax.fori_loop(0, slots, step, found, unroll=4)
    for extra in range(GROUP):
        slot_of[found + extra] = len(lists) * slots
        source_of[found + extra] = 0
        target_of[found + extra] = 0
    return (found + GROUP - 1) // GROUP


def load_links(links, held, sem):
    slots = links[0].shape[0]
    copies = []
    for number, ref in enumerate(links):
        copies.append(
            pltpu.make_async_copy(ref, held.at[pl.ds(number * slots, slots)], sem.at[number])
        )
    for copy in copies:
        copy.start()
    tail = len(links) * slots
    held[tail:, :] = jnp.full((held.shape[0] - tail, TILE), -1, jnp.int32)
    return copies


def hop_one_kernel(n_item, n_edge, half_tiles, *refs):
    lists = [refs[3 * e : 3 * e + 3] for e in range(n_edge)]
    refs = refs[3 * n_edge :]
    links, refs = refs[:n_edge], refs[n_edge:]
    items, refs = refs[0], refs[1:]
    pieces, refs = refs[: 2 * n_item], refs[2 * n_item :]
    degree, total, held, rows, slot_of, source_of, target_of, sem = refs
    slots = links[0].shape[0]
    me, core = lax.axis_index("item"), lax.axis_index("edge")
    copies = load_links(links, held, sem)
    copies.append(pltpu.make_async_copy(items, rows, sem.at[n_edge]))
    copies[-1].start()

    def pick(item, user):
        target = user - core * half_tiles
        return item, target, jnp.logical_and(target >= 0, target < half_tiles)

    groups = choose_slots(lists, slots, pick, slot_of, source_of, target_of)
    total[...] = jnp.zeros_like(total)
    degree[...] = jnp.zeros_like(degree)
    for copy in copies:
        copy.wait()
    inside = lax.broadcasted_iota(jnp.int32, (TILE, TILE), 0)
    ones = jnp.ones((8, TILE), BF16)

    def step(g, carry):
        for i in range(GROUP):
            at = g * GROUP + i
            link = held[pl.ds(slot_of[at], 1), :]
            onehot = jnp.where(inside == link, 1.0, 0.0).astype(BF16)
            source = pl.multiple_of(source_of[at] * TILE, TILE)
            target = pl.multiple_of(target_of[at] * TILE, TILE)
            part = jnp.dot(onehot, rows[pl.ds(source, TILE), :], preferred_element_type=F32)
            total[pl.ds(target, TILE), :] += part
            hits = lax.dot_general(
                ones, onehot, (((1,), (1,)), ((), ())), preferred_element_type=F32
            )
            low = pl.multiple_of(target_of[at] * 8, 8)
            degree[pl.ds(low, 8), :] += hits
        return carry

    lax.fori_loop(0, groups, step, 0)
    span = total.shape[0] // n_item
    for k in range(n_item):
        owner = jnp.bitwise_xor(me, k)
        for h in range(2):
            first = pl.multiple_of(owner * span + h * (span // 2), 16)
            out = pieces[2 * k + h]
            out[...] = total[pl.ds(first, span // 2), :].astype(out.dtype)


def hop_one(lists, links, items, n_item, n_edge, user_tiles):
    half_tiles = user_tiles // n_edge
    slots, channels = links[0].shape[0], items.shape[1]
    piece = half_tiles * TILE // n_item // 2
    shapes = [
        jax.ShapeDtypeStruct((piece, channels), F32 if k == 0 else BF16)
        for k in range(n_item)
        for _ in range(2)
    ]
    shapes.append(jax.ShapeDtypeStruct((half_tiles * 8, TILE), F32))
    room = n_edge * slots + GROUP
    return pl.pallas_call(
        functools.partial(hop_one_kernel, n_item, n_edge, half_tiles),
        out_shape=shapes,
        in_specs=[SMEM] * (3 * n_edge) + [ANY] * (n_edge + 1),
        out_specs=[VMEM] * len(shapes),
        scratch_shapes=[
            pltpu.VMEM((half_tiles * TILE, channels), F32),
            pltpu.VMEM((n_edge * slots + 8, TILE), jnp.int32),
            pltpu.VMEM(items.shape, BF16),
            pltpu.SMEM((room,), jnp.int32),
            pltpu.SMEM((room,), jnp.int32),
            pltpu.SMEM((room,), jnp.int32),
            pltpu.SemaphoreType.DMA((n_edge + 1,)),
        ],
        name="hop_one",
    )(*[part for entry in lists for part in entry], *links, items)


def refresh_body(counts, n_degree, half_tiles, *refs):
    low = refs[: counts[0]]
    refs = refs[counts[0] :]
    high = refs[: counts[1]]
    refs = refs[counts[1] :]
    degrees, refs = refs[:n_degree], refs[n_degree:]
    weight, emb, out_low, out_high, own, inverse, sem = refs
    me, core = lax.axis_index("item"), lax.axis_index("edge")
    piece = out_low.shape[0]
    first = core * half_tiles * TILE + me * 2 * piece
    copy = pltpu.make_async_copy(emb.at[pl.ds(pl.multiple_of(first, 16), 2 * piece)], own, sem)
    copy.start()
    degree = degrees[0][...]
    for other in degrees[1:]:
        degree = degree + other[...]
    scale = 1.0 / jnp.maximum(degree, 1.0)
    for t in range(half_tiles):
        row = jnp.broadcast_to(scale[t * 8 : t * 8 + 1, :], (TILE, TILE))
        inverse[t * TILE : (t + 1) * TILE, :] = row.T
    copy.wait()
    for h, (group, out) in enumerate(((low, out_low), (high, out_high))):
        summed = group[0][...]
        for other in group[1:]:
            summed = summed + other[...].astype(F32)
        at = pl.multiple_of(me * 2 * piece + h * piece, 8)
        factor = inverse[pl.ds(at, piece), :]
        width = summed.shape[1] // TILE
        mean = (summed * jnp.concatenate([factor] * width, axis=1)).astype(BF16)
        projected = jnp.dot(mean, weight[...], preferred_element_type=F32)
        kept = own[h * piece : (h + 1) * piece, :].astype(F32)
        out[...] = (kept + silu(projected)).astype(BF16)


def refresh(low, high, degrees, weight, user_emb, n_edge):
    piece, channels = low[0].shape
    half_tiles = user_emb.shape[0] // TILE // n_edge
    shape = jax.ShapeDtypeStruct((piece, channels), BF16)
    count = len(low) + len(high) + len(degrees) + 1
    return pl.pallas_call(
        functools.partial(refresh_body, (len(low), len(high)), len(degrees), half_tiles),
        out_shape=[shape, shape],
        in_specs=[VMEM] * count + [ANY],
        out_specs=[VMEM] * 2,
        scratch_shapes=[
            pltpu.VMEM((2 * piece, channels), BF16),
            pltpu.VMEM((half_tiles * TILE, TILE), F32),
            pltpu.SemaphoreType.DMA(()),
        ],
        name="refresh",
    )(*low, *high, *degrees, weight, user_emb)


def chunk_order(place, n_user):
    if n_user == 4:
        upper = place >= 2
        return [place, jnp.bitwise_xor(place, 1), jnp.where(upper, 1, 2), jnp.where(upper, 0, 3)]
    return [jnp.bitwise_xor(place, k) for k in range(n_user)]


def hop_two_kernel(n_item, n_user, n_edge, item_tiles, *refs):
    lists = [refs[3 * e : 3 * e + 3] for e in range(n_edge)]
    refs = refs[3 * n_edge :]
    links, refs = refs[:n_edge], refs[n_edge:]
    total_pieces = n_edge * n_item * 2
    pieces, refs = refs[:total_pieces], refs[total_pieces:]
    outs, refs = refs[:n_user], refs[n_user:]
    counts, total, held, rows, slot_of, source_of, target_of, sem = refs
    slots = links[0].shape[0]
    me, core, place = lax.axis_index("item"), lax.axis_index("edge"), lax.axis_index("user")
    share = item_tiles // (n_user * n_edge)
    piece = pieces[0].shape[0]
    copies = load_links(links, held, sem)
    for d in range(n_edge):
        for k in range(n_item):
            for h in range(2):
                number = (d * n_item + k) * 2 + h
                owner = jnp.bitwise_xor(core, d) * n_item + jnp.bitwise_xor(me, k)
                first = pl.multiple_of((owner * 2 + h) * piece, 16)
                copies.append(
                    pltpu.make_async_copy(
                        pieces[number], rows.at[pl.ds(first, piece)], sem.at[n_edge + number]
                    )
                )
                copies[-1].start()

    def pick(item, user):
        whose = item // share
        target = (whose // n_edge) * share + item % share
        return user, target, whose % n_edge == core

    groups = choose_slots(lists, slots, pick, slot_of, source_of, target_of)
    for t in range(item_tiles):
        counts[t] = 0
    for items, _, count in lists:

        def tally(b, carry, items=items):
            counts[items[b]] += 1
            return carry

        lax.fori_loop(0, count[0], tally, 0)
    total[...] = jnp.zeros_like(total)
    for copy in copies:
        copy.wait()
    inside = lax.broadcasted_iota(jnp.int32, (TILE, TILE), 0)

    def step(g, carry):
        for i in range(GROUP):
            at = g * GROUP + i
            link = held[pl.ds(slot_of[at], 1), :]
            onehot = jnp.where(inside == link, 1.0, 0.0).astype(BF16)
            source = pl.multiple_of(source_of[at] * TILE, TILE)
            target = pl.multiple_of(target_of[at] * TILE, TILE)
            part = lax.dot_general(
                onehot,
                rows[pl.ds(source, TILE), :],
                (((0,), (0,)), ((), ())),
                preferred_element_type=F32,
            )
            total[pl.ds(target, TILE), :] += part
        return carry

    lax.fori_loop(0, groups, step, 0)
    span = share * TILE
    for out, chunk in zip(outs, chunk_order(place, n_user)):
        first = pl.multiple_of(chunk * span, span)
        out[...] = total[pl.ds(first, span), :].astype(out.dtype)


def hop_two(lists, links, pieces, n_item, n_user, n_edge, item_tiles):
    slots, channels = links[0].shape[0], pieces[0].shape[1]
    users = len(pieces) * pieces[0].shape[0]
    span = item_tiles // (n_user * n_edge) * TILE
    shapes = [
        jax.ShapeDtypeStruct((span, channels), F32 if k == 0 else BF16) for k in range(n_user)
    ]
    shapes.append(jax.ShapeDtypeStruct((item_tiles,), jnp.int32))
    room = n_edge * slots + GROUP
    return pl.pallas_call(
        functools.partial(hop_two_kernel, n_item, n_user, n_edge, item_tiles),
        out_shape=shapes,
        in_specs=[SMEM] * (3 * n_edge) + [ANY] * (n_edge + len(pieces)),
        out_specs=[VMEM] * n_user + [SMEM],
        scratch_shapes=[
            pltpu.VMEM((n_user * span, channels), F32),
            pltpu.VMEM((n_edge * slots + 8, TILE), jnp.int32),
            pltpu.VMEM((users, channels), BF16),
            pltpu.SMEM((room,), jnp.int32),
            pltpu.SMEM((room,), jnp.int32),
            pltpu.SMEM((room,), jnp.int32),
            pltpu.SemaphoreType.DMA((n_edge + len(pieces),)),
        ],
        name="hop_two",
    )(*[part for entry in lists for part in entry], *links, *pieces)


def finish_kernel(n_sums, n_counts, n_edge, *refs):
    sums, refs = refs[:n_sums], refs[n_sums:]
    counts, refs = refs[:n_counts], refs[n_counts:]
    up, down, emb, out, own, sem = refs
    place = lax.axis_index("user") * n_edge + lax.axis_index("edge")
    span = out.shape[0]
    copy = pltpu.make_async_copy(
        emb.at[pl.ds(pl.multiple_of(place * span, span), span)], own, sem
    )
    copy.start()
    copy.wait()
    for t in range(span // TILE):
        rows = slice(t * TILE, (t + 1) * TILE)
        number = counts[0][place * (span // TILE) + t]
        for other in counts[1:]:
            number = number + other[place * (span // TILE) + t]
        degree = jnp.full((TILE, 1), jnp.maximum(number, 1), jnp.int32).astype(F32)
        summed = sums[0][rows, :]
        for other in sums[1:]:
            summed = summed + other[rows, :].astype(F32)
        merged = own[rows, :].astype(F32) + summed / degree
        hidden = silu(jnp.dot(merged.astype(BF16), up[...], preferred_element_type=F32))
        added = jnp.dot(hidden.astype(BF16), down[...], preferred_element_type=F32)
        out[rows, :] = (merged + added).astype(BF16)


def finish(sums, counts, up, down, item_emb, n_edge):
    span, channels = sums[0].shape
    return pl.pallas_call(
        functools.partial(finish_kernel, len(sums), len(counts), n_edge),
        out_shape=jax.ShapeDtypeStruct((span, channels), BF16),
        in_specs=[VMEM] * len(sums) + [SMEM] * len(counts) + [VMEM, VMEM, ANY],
        out_specs=VMEM,
        scratch_shapes=[pltpu.VMEM((span, channels), BF16), pltpu.SemaphoreType.DMA(())],
        name="finish",
    )(*sums, *counts, up, down, item_emb)


def swap(value, axis, size, k):
    return lax.ppermute(value, axis, [(i, i ^ k) for i in range(size)])


def add(a, b):
    return (a.astype(F32) + b.astype(F32)).astype(BF16)


def doubled(value, axis, size):
    k, other = 1, None
    while k < size:
        if other is not None:
            value = value + other
        other = swap(value, axis, size, k)
        k *= 2
    return [value] if other is None else [value, other]


def gather_sums(pieces, size):
    if size == 4:
        (own_low, own_high), (x_low, x_high), (y_low, y_high), (d_low, d_high) = pieces
        move = lambda value, k: swap(value, "item", size, k)
        a1, b1 = move(d_low, 1), move(d_high, 2)
        a2, b2 = move(x_low, 1), move(y_high, 2)
        r1, r2 = move(add(y_low, a1), 2), move(add(x_high, b1), 1)
        return [own_low, a2, r1], [own_high, b2, r2]
    low, high = [pieces[0][0]], [pieces[0][1]]
    for k in range(1, size):
        low.append(swap(pieces[k][0], "item", size, k))
        high.append(swap(pieces[k][1], "item", size, k))
    return low, high


def spread(low, high, size):
    move = lambda value, k: swap(value, "item", size, k)
    if size == 4:
        x_low, y_high = move(low, 1), move(high, 2)
        x_high, y_low = move(high, 1), move(low, 2)
        d_low, d_high = move(x_low, 2), move(y_high, 1)
        return [low, high, x_low, x_high, y_low, y_high, d_low, d_high]
    out = [low, high]
    for k in range(1, size):
        out += [move(low, k), move(high, k)]
    return out


def collect_items(chunks, size):
    move = lambda value, pairs: lax.ppermute(value, "user", pairs)
    if size == 4:
        own, pair, cross, far = chunks
        first = move(far, [(0, 1), (3, 2)])
        near = move(cross, [(1, 2), (2, 1)])
        side = swap(pair, "user", size, 1)
        long = move(cross, [(0, 2), (3, 1)])
        last = move(add(far, first), [(1, 3), (2, 0)])
        return [own, near, side, long, last]
    return [chunks[0]] + [swap(chunks[k], "user", size, k) for k in range(1, size)]


def body(
    sizes,
    item_emb,
    user_emb,
    block_item,
    block_user,
    block_rows,
    block_count,
    user_weight,
    up_weight,
    down_weight,
):
    n_item, n_user, n_edge = sizes
    item_tiles = item_emb.shape[0] // TILE
    user_tiles = user_emb.shape[0] // TILE
    mine = (block_item.reshape(-1), block_user.reshape(-1), block_count.reshape(-1))
    mine_links = block_rows.reshape(-1, TILE)
    lists, links = [mine], [mine_links]
    for k in range(1, n_edge):
        lists.append(tuple(swap(part, "edge", n_edge, k) for part in mine))
        links.append(swap(mine_links, "edge", n_edge, k))
    *parts, hits = hop_one(lists, links, item_emb, n_item, n_edge, user_tiles)
    parts = [tuple(parts[2 * k : 2 * k + 2]) for k in range(n_item)]
    low, high = gather_sums(parts, n_item)
    degrees = doubled(hits, "item", n_item)
    new_low, new_high = refresh(low, high, degrees, user_weight, user_emb, n_edge)
    pieces = spread(new_low, new_high, n_item)
    everything = list(pieces)
    for k in range(1, n_edge):
        everything += [swap(piece, "edge", n_edge, k) for piece in pieces]
    *chunks, tally = hop_two(lists, links, everything, n_item, n_user, n_edge, item_tiles)
    sums = collect_items(chunks, n_user)
    counts = doubled(tally, "user", n_user)
    return finish(sums, counts, up_weight, down_weight, item_emb, n_edge)


def solution(mesh):
    sizes = tuple(mesh.shape[name] for name in ("item", "user", "edge"))
    return jax.shard_map(
        functools.partial(body, sizes),
        mesh=mesh,
        in_specs=(
            P("item", None),
            P("user", None),
            P("item", "user", "edge", None),
            P("item", "user", "edge", None),
            P("item", "user", "edge", None, None),
            P("item", "user", "edge"),
            P(),
            P(),
            P(),
        ),
        out_specs=P(("item", "user", "edge"), None),
        check_vma=False,
    )
```

time: 276 us -> 104 us (0.38)
  waiting for transfers between devices: 90 us -> 30.4 us
  local copies, waits for them, and re-layouts: 58.7 us -> 2.85 us
  blocking collectives: 53 us -> 0 us
  matrix products: 51 us -> 0 us
  starting transfers between devices: 0.09 us -> 37.7 us
  Pallas kernels: 0 us -> 27.5 us
  between operations: 15.2 us -> 1.05 us
  other arithmetic: 7.5 us -> 4.5 us
    reduce_scatter x2 -> x0, waiting for transfers between devices: 57.7 us -> none  [the longest x1 36.6 us: body(): lax.psum_scatter(user_part, ('item', 'edge'), scatter_dimension=0, tiled=...]
    unnamed x2 -> x0, blocking collectives: 53 us -> none
    dot_general x17 -> x0, matrix products: 51 us -> none  [the longest x3 19.6 us: first_hop(): jnp.einsum('sg,gcd->scd', chooser, contrib, precision=lax.Precision.HIGHEST)]
    ppermute x0 -> x33, starting transfers between devices: none -> 37.7 us  [the longest x29 28.3 us: swap(): return lax.ppermute(value, axis, [(i, i ^ k) for i in range(size)])]
    while x26 -> x0, local copies, waits for them, and re-layouts: 35.2 us -> none
    all_gather x1 -> x0, waiting for transfers between devices: 32.3 us -> none  [body(): user_new = lax.all_gather(mine, ('item', 'edge'), axis=0, tiled=True)]
    ppermute x0 -> x33, waiting for transfers between devices: none -> 30.4 us  [the longest x29 28.7 us: swap(): return lax.ppermute(value, axis, [(i, i ^ k) for i in range(size)])]
    pallas_call x0 -> x4, Pallas kernels: none -> 27.5 us  [the longest x1 10.8 us: hop_two(): pl.pallas_call(functools.partial(hop_two_kernel, n_item, n_user, n_edge,...]
  transfers between devices with their start and end apart: 3 -> 33, of which waited for: 3 -> 14; matrix products, arithmetic and copies ran while one was open for 1% -> 4% of each run, Pallas kernels for 0% -> 0%
where the time goes in v1:
time: 104 us
  starting transfers between devices  37.7 us (36%)
  waiting for transfers between devices  30.4 us (29%)
  Pallas kernels  27.5 us (26%)
  other arithmetic  4.5 us (4%)
  local copies, waits for them, and re-layouts  2.85 us (3%)
  between operations  1.05 us (1%)
    ppermute x29, waiting for transfers between devices, swap(): return lax.ppermute(value, axis, [(i, i ^ k) for i in range(size)])  28.7 us
    ppermute x29, starting transfers between devices, swap(): return lax.ppermute(value, axis, [(i, i ^ k) for i in range(size)])  28.3 us
    pallas_call x1, Pallas kernels, hop_two(): pl.pallas_call(functools.partial(hop_two_kernel, n_item, n_user, n_edge,...  10.8 us
    ppermute x4, starting transfers between devices, collect_items(): move = lambda value, pairs: lax.ppermute(value, 'user', pairs)  9.36 us
    pallas_call x1, Pallas kernels, hop_one(): pl.pallas_call(functools.partial(hop_one_kernel, n_item, n_edge, half_til...  8.61 us
    pallas_call x1, Pallas kernels, finish(): pl.pallas_call(functools.partial(finish_kernel, len(sums), len(counts), n...  4.37 us
    pallas_call x1, Pallas kernels, refresh(): pl.pallas_call(functools.partial(refresh_body, (len(low), len(high)), len...  3.66 us
    convert_element_type x3, other arithmetic, add(): return (a.astype(F32) + b.astype(F32)).astype(BF16)  2.98 us
  transfers between devices with their start and end apart: 33, of which 14 were waited for; matrix products, arithmetic and copies ran while one was open for 4% of the time, Pallas kernels for 0%

profile of v1, /device:TPU:0, one launch (start us, length us, event | category | flops | bytes accessed | tf_op | source)
XLA Modules:
  0.0 103.9 jit_solution(14914063555974860788)
XLA Ops:
  2.9 8.6 %hop_one.1 = (f32[384,256]{1,0:T(8,128)}, f32[384,256]{1,0:T(8,128)}, bf16[384,256]{1,0:T(8,128)(2,1)}, bf16[384,256]{1,0:T(8,128)(2,1)}, bf16[384,256]{1,0:T(8,...) custom-call(s32[96]{0:T(128)} %bitcast.10, ...), custom_call_target="tpu_custom_call" | custom-call | tf_op jit(solution)/shard_map/hop_one/pallas_call | solution.py:119
  11.5 2.3 %collective-permute-start.5 = (bf16[384,256]{1,0:T(8,128)(2,1)}, bf16[384,256]{1,0:T(8,128)(2,1)S(1)}, u32[]{:S(2)}, u32[]{:S(2)}) collective-permute-start(bf16[384,256]{1,0:T(8,128)(2,1)} %get-tuple-element.24), channel_id=1, source_target_pairs={{0,8},{8,0},{16,24},{24,16},{1,9},{9,1},{17,25},{25,17},{2,10},{10... | collective-permute-start | bytes 589832 | tf_op jit(solution)/shard_map/ppermute | solution.py:331
  13.9 1.9 %collective-permute-start.4 = (bf16[384,256]{1,0:T(8,128)(2,1)}, bf16[384,256]{1,0:T(8,128)(2,1)S(1)}, u32[]{:S(2)}, u32[]{:S(2)}) collective-permute-start(bf16[384,256]{1,0:T(8,128)(2,1)} %get-tuple-element.22), channel_id=1, source_target_pairs={{0,8},{8,0},{16,24},{24,16},{1,9},{9,1},{17,25},{25,17},{2,10},{10... | collective-permute-start | bytes 589832 | tf_op jit(solution)/shard_map/ppermute | solution.py:331
  15.9 2.0 %collective-permute-start.8 = (bf16[384,256]{1,0:T(8,128)(2,1)}, bf16[384,256]{1,0:T(8,128)(2,1)S(1)}, u32[]{:S(2)}, u32[]{:S(2)}) collective-permute-start(bf16[384,256]{1,0:T(8,128)(2,1)} %get-tuple-element.28), channel_id=1, source_target_pairs={{0,16},{8,24},{16,0},{24,8},{1,17},{9,25},{17,1},{25,9},{2,18},{10... | collective-permute-start | bytes 589832 | tf_op jit(solution)/shard_map/ppermute | solution.py:331
  19.9 2.6 %collective-permute-start.6 = (bf16[384,256]{1,0:T(8,128)(2,1)S(1)}, bf16[384,256]{1,0:T(8,128)(2,1)S(1)}, u32[]{:S(2)}, u32[]{:S(2)}) collective-permute-start(bf16[384,256]{1,0:T(8,128)(2,1)S(1)} %add_convert_fusion.2), channel_id=1, source_target_pairs={{0,16},{8,24},{16,0},{24,8},{1,17},{9,25},{17,1},{25,9},{2,18},{10... | collective-permute-start | bytes 589832 | tf_op jit(solution)/shard_map/ppermute | solution.py:331
  22.5 5.6 %collective-permute-done.8 = bf16[384,256]{1,0:T(8,128)(2,1)S(1)} collective-permute-done((bf16[384,256]{1,0:T(8,128)(2,1)}, bf16[384,256]{1,0:T(8,128)(2,1)S(1)}, u32[]{:S(2)}, u32[]{:S(2)}) %collective-permute-start.8) | collective-permute-done | bytes 196640 | tf_op jit(solution)/shard_map/ppermute | solution.py:331
  30.1 1.7 %collective-permute-start.11 = (f32[192,128]{1,0:T(8,128)S(1)}, f32[192,128]{1,0:T(8,128)S(1)}, u32[]{:S(2)}, u32[]{:S(2)}) collective-permute-start(f32[192,128]{1,0:T(8,128)S(1)} %add.17.refs_6_), channel_id=1, source_target_pairs={{0,16},{8,24},{16,0},{24,8},{1,17},{9,25},{17,1},{25,9},{2,18},{10... | collective-permute-start | bytes 294920 | tf_op jit(solution)/shard_map/ppermute | solution.py:331
  31.8 3.0 %collective-permute-done.11.refs_7_ = f32[192,128]{1,0:T(8,128)S(1)} collective-permute-done((f32[192,128]{1,0:T(8,128)S(1)}, f32[192,128]{1,0:T(8,128)S(1)}, u32[]{:S(2)}, u32[]{:S(2)}) %collective-permute-start.11) | collective-permute-done | bytes 98336 | tf_op jit(solution)/shard_map/ppermute | solution.py:331
  36.2 3.7 %refresh.1 = (bf16[384,256]{1,0:T(8,128)(2,1)}, bf16[384,256]{1,0:T(8,128)(2,1)}) custom-call(f32[384,256]{1,0:T(8,128)} %get-tuple-element.21.refs_0_, bf16[384,256]{1,0:T(8,128)(2,1)} %copy-done.5, bf16[384,256]{1,0:T(8,128)(2,1)} %copy-done.7, f32[384,256]{1,0:T(8,128)} %get-tuple-element.25.refs_3_, bf16[384,256]{1,0:T(8,128)(2,1)} %copy-done.6, ...), custom_call_target="tpu_custom_call" | custom-call | tf_op jit(solution)/shard_map/refresh/pallas_call | solution.py:175
  41.6 1.9 %collective-permute-start.15 = (bf16[384,256]{1,0:T(8,128)(2,1)}, bf16[384,256]{1,0:T(8,128)(2,1)S(1)}, u32[]{:S(2)}, u32[]{:S(2)}) collective-permute-start(bf16[384,256]{1,0:T(8,128)(2,1)} %get-tuple-element.31.refs_9_), channel_id=1, source_target_pairs={{0,16},{8,24},{16,0},{24,8},{1,17},{9,25},{17,1},{25,9},{2,18},{10... | collective-permute-start | bytes 589832 | tf_op jit(solution)/shard_map/ppermute | solution.py:331
  44.2 3.9 %collective-permute-done.14.refs_12_ = bf16[384,256]{1,0:T(8,128)(2,1)S(1)} collective-permute-done((bf16[384,256]{1,0:T(8,128)(2,1)}, bf16[384,256]{1,0:T(8,128)(2,1)S(1)}, u32[]{:S(2)}, u32[]{:S(2)}) %collective-permute-start.14) | collective-permute-done | bytes 196640 | tf_op jit(solution)/shard_map/ppermute | solution.py:331
  50.1 2.2 %collective-permute-done.15.refs_13_ = bf16[384,256]{1,0:T(8,128)(2,1)S(1)} collective-permute-done((bf16[384,256]{1,0:T(8,128)(2,1)}, bf16[384,256]{1,0:T(8,128)(2,1)S(1)}, u32[]{:S(2)}, u32[]{:S(2)}) %collective-permute-start.15) | collective-permute-done | bytes 196640 | tf_op jit(solution)/shard_map/ppermute | solution.py:331
  52.3 1.4 %collective-permute-start.17 = (bf16[384,256]{1,0:T(8,128)(2,1)S(1)}, bf16[384,256]{1,0:T(8,128)(2,1)S(1)}, u32[]{:S(2)}, u32[]{:S(2)}) collective-permute-start(bf16[384,256]{1,0:T(8,128)(2,1)S(1)} %collective-permute-done.15.refs_13_), channel_id=1, source_target_pairs={{0,8},{8,0},{16,24},{24,16},{1,9},{9,1},{17,25},{25,17},{2,10},{10... | collective-permute-start | bytes 589832 | tf_op jit(solution)/shard_map/ppermute | solution.py:331
  54.3 1.6 %collective-permute-done.16.refs_14_ = bf16[384,256]{1,0:T(8,128)(2,1)S(1)} collective-permute-done((bf16[384,256]{1,0:T(8,128)(2,1)S(1)}, bf16[384,256]{1,0:T(8,128)(2,1)S(1)}, u32[]{:S(2)}, u32[]{:S(2)}) %collective-permute-start.16) | collective-permute-done | bytes 196640 | tf_op jit(solution)/shard_map/ppermute | solution.py:331
  55.9 2.2 %collective-permute-done.17.refs_15_ = bf16[384,256]{1,0:T(8,128)(2,1)S(1)} collective-permute-done((bf16[384,256]{1,0:T(8,128)(2,1)S(1)}, bf16[384,256]{1,0:T(8,128)(2,1)S(1)}, u32[]{:S(2)}, u32[]{:S(2)}) %collective-permute-start.17) | collective-permute-done | bytes 196640 | tf_op jit(solution)/shard_map/ppermute | solution.py:331
  60.2 10.8 %hop_two.1 = (f32[512,256]{1,0:T(8,128)}, bf16[512,256]{1,0:T(8,128)(2,1)}, bf16[512,256]{1,0:T(8,128)(2,1)}, bf16[512,256]{1,0:T(8,128)(2,1)}, s32[32]{0:T(128)}) custom-call(s32[96]{0:T(128)} %bitcast.11, s32[96]{0:T(128)} %bitcast.14, s32[1]{0:T(128)} %bitcast.5.refs_2_, s32[96]{0:T(128)} %copy-done.25, s32[96]{0:T(128)} %copy-done.26, ...), custom_call_target="tpu_custom_call" | custom-call | tf_op jit(solution)/shard_map/hop_two/pallas_call | solution.py:274
  71.1 4.0 %collective-permute-start.29 = (bf16[512,256]{1,0:T(8,128)(2,1)}, bf16[512,256]{1,0:T(8,128)(2,1)S(1)}, u32[]{:S(2)}, u32[]{:S(2)}) collective-permute-start(bf16[512,256]{1,0:T(8,128)(2,1)} %get-tuple-element.35), channel_id=1, source_target_pairs={{0,2},{6,4},{1,3},{7,5},{8,10},{14,12},{9,11},{15,13},{16,18},{22,... | collective-permute-start | bytes 786440 | tf_op jit(solution)/shard_map/ppermute | solution.py:377
  75.0 3.4 %collective-permute-start.28 = (bf16[512,256]{1,0:T(8,128)(2,1)}, bf16[512,256]{1,0:T(8,128)(2,1)S(1)}, u32[]{:S(2)}, u32[]{:S(2)}) collective-permute-start(bf16[512,256]{1,0:T(8,128)(2,1)} %get-tuple-element.33), channel_id=1, source_target_pairs={{0,4},{6,2},{1,5},{7,3},{8,12},{14,10},{9,13},{15,11},{16,20},{22,... | collective-permute-start | bytes 786440 | tf_op jit(solution)/shard_map/ppermute | solution.py:377
  80.4 1.6 %collective-permute-done.29 = bf16[512,256]{1,0:T(8,128)(2,1)S(1)} collective-permute-done((bf16[512,256]{1,0:T(8,128)(2,1)}, bf16[512,256]{1,0:T(8,128)(2,1)S(1)}, u32[]{:S(2)}, u32[]{:S(2)}) %collective-permute-start.29) | collective-permute-done | bytes 262176 | tf_op jit(solution)/shard_map/ppermute | solution.py:377
  84.3 4.8 %collective-permute-start.31 = (s32[32]{0:T(128)}, s32[32]{0:T(128)S(1)}, u32[]{:S(2)}, u32[]{:S(2)}) collective-permute-start(s32[32]{0:T(128)} %get-tuple-element.36), channel_id=1, source_target_pairs={{0,2},{2,0},{4,6},{6,4},{1,3},{3,1},{5,7},{7,5},{8,10},{10,8},{12,... | collective-permute-start | bytes 392 | tf_op jit(solution)/shard_map/ppermute | solution.py:331
  89.2 4.0 %collective-permute-done.31 = s32[32]{0:T(128)S(1)} collective-permute-done((s32[32]{0:T(128)}, s32[32]{0:T(128)S(1)}, u32[]{:S(2)}, u32[]{:S(2)}) %collective-permute-start.31) | collective-permute-done | bytes 160 | tf_op jit(solution)/shard_map/ppermute | solution.py:331
  93.8 3.2 %collective-permute-start.32 = (s32[32]{0:T(128)S(1)}, s32[32]{0:T(128)S(1)}, u32[]{:S(2)}, u32[]{:S(2)}) collective-permute-start(s32[32]{0:T(128)S(1)} %add.19.refs_5_), channel_id=1, source_target_pairs={{0,4},{2,6},{4,0},{6,2},{1,5},{3,7},{5,1},{7,3},{8,12},{10,14},{12... | collective-permute-start | bytes 392 | tf_op jit(solution)/shard_map/ppermute | solution.py:331
  97.0 1.5 %collective-permute-done.32.refs_6_ = s32[32]{0:T(128)S(1)} collective-permute-done((s32[32]{0:T(128)S(1)}, s32[32]{0:T(128)S(1)}, u32[]{:S(2)}, u32[]{:S(2)}) %collective-permute-start.32) | collective-permute-done | bytes 160 | tf_op jit(solution)/shard_map/ppermute | solution.py:331
  99.5 4.4 %finish.1 = bf16[512,256]{1,0:T(8,128)(2,1)} custom-call(f32[512,256]{1,0:T(8,128)} %get-tuple-element.32.refs_0_, bf16[512,256]{1,0:T(8,128)(2,1)} %copy-done.2, bf16[512,256]{1,0:T(8,128)(2,1)} %copy-done.3, bf16[512,256]{1,0:T(8,128)(2,1)} %copy-done.1, bf16[512,256]{1,0:T(8,128)(2,1)} %copy-done.4, s32[32]{0:T(128)} %copy-done.27, s32[32]{0:T(128)} %copy-done.28, ...), custom_call_target="tpu_custom_call" | custom-call | tf_op jit(solution)/shard_map/finish/pallas_call | solution.py:320
  (109 shorter events, 20.5 us)
Async XLA Ops:
  11.5 7.4 %collective-permute-start.5 = (bf16[384,256]{1,0:T(8,128)(2,1)}, bf16[384,256]{1,0:T(8,128)(2,1)S(1)}, u32[]{:S(2)}, u32[]{:S(2)}) collective-permute-start(bf16[384,256]{1,0:T(8,128)(2,1)} %get-tuple-element.24), channel_id=1, source_target_pairs={{0,8},{8,0},{16,24},{24,16},{1,9},{9,1},{17,25},{25,17},{2,10},{10... | collective-permute-start | bytes 589832 | tf_op jit(solution)/shard_map/ppermute | solution.py:331
  13.9 15.3 %collective-permute-start.10 = (f32[192,128]{1,0:T(8,128)}, f32[192,128]{1,0:T(8,128)S(1)}, u32[]{:S(2)}, u32[]{:S(2)}) collective-permute-start(f32[192,128]{1,0:T(8,128)} %get-tuple-element.29), channel_id=1, source_target_pairs={{0,8},{8,0},{16,24},{24,16},{1,9},{9,1},{17,25},{25,17},{2,10},{10... | collective-permute-start | bytes 294920 | tf_op jit(solution)/shard_map/ppermute | solution.py:331
  13.9 20.9 %collective-permute-start.4 = (bf16[384,256]{1,0:T(8,128)(2,1)}, bf16[384,256]{1,0:T(8,128)(2,1)S(1)}, u32[]{:S(2)}, u32[]{:S(2)}) collective-permute-start(bf16[384,256]{1,0:T(8,128)(2,1)} %get-tuple-element.22), channel_id=1, source_target_pairs={{0,8},{8,0},{16,24},{24,16},{1,9},{9,1},{17,25},{25,17},{2,10},{10... | collective-permute-start | bytes 589832 | tf_op jit(solution)/shard_map/ppermute | solution.py:331
  15.9 18.9 %collective-permute-start.7 = (bf16[384,256]{1,0:T(8,128)(2,1)}, bf16[384,256]{1,0:T(8,128)(2,1)S(1)}, u32[]{:S(2)}, u32[]{:S(2)}) collective-permute-start(bf16[384,256]{1,0:T(8,128)(2,1)} %get-tuple-element.26), channel_id=1, source_target_pairs={{0,16},{8,24},{16,0},{24,8},{1,17},{9,25},{17,1},{25,9},{2,18},{10... | collective-permute-start | bytes 589832 | tf_op jit(solution)/shard_map/ppermute | solution.py:331
  15.9 12.2 %collective-permute-start.8 = (bf16[384,256]{1,0:T(8,128)(2,1)}, bf16[384,256]{1,0:T(8,128)(2,1)S(1)}, u32[]{:S(2)}, u32[]{:S(2)}) collective-permute-start(bf16[384,256]{1,0:T(8,128)(2,1)} %get-tuple-element.28), channel_id=1, source_target_pairs={{0,16},{8,24},{16,0},{24,8},{1,17},{9,25},{17,1},{25,9},{2,18},{10... | collective-permute-start | bytes 589832 | tf_op jit(solution)/shard_map/ppermute | solution.py:331
  19.9 14.9 %collective-permute-start.6 = (bf16[384,256]{1,0:T(8,128)(2,1)S(1)}, bf16[384,256]{1,0:T(8,128)(2,1)S(1)}, u32[]{:S(2)}, u32[]{:S(2)}) collective-permute-start(bf16[384,256]{1,0:T(8,128)(2,1)S(1)} %add_convert_fusion.2), channel_id=1, source_target_pairs={{0,16},{8,24},{16,0},{24,8},{1,17},{9,25},{17,1},{25,9},{2,18},{10... | collective-permute-start | bytes 589832 | tf_op jit(solution)/shard_map/ppermute | solution.py:331
  29.1 6.5 %collective-permute-start.9 = (bf16[384,256]{1,0:T(8,128)(2,1)S(1)}, bf16[384,256]{1,0:T(8,128)(2,1)S(1)}, u32[]{:S(2)}, u32[]{:S(2)}) collective-permute-start(bf16[384,256]{1,0:T(8,128)(2,1)S(1)} %add_convert_fusion.1), channel_id=1, source_target_pairs={{0,8},{8,0},{16,24},{24,16},{1,9},{9,1},{17,25},{25,17},{2,10},{10... | collective-permute-start | bytes 589832 | tf_op jit(solution)/shard_map/ppermute | solution.py:331
  30.1 4.7 %collective-permute-start.11 = (f32[192,128]{1,0:T(8,128)S(1)}, f32[192,128]{1,0:T(8,128)S(1)}, u32[]{:S(2)}, u32[]{:S(2)}) collective-permute-start(f32[192,128]{1,0:T(8,128)S(1)} %add.17.refs_6_), channel_id=1, source_target_pairs={{0,16},{8,24},{16,0},{24,8},{1,17},{9,25},{17,1},{25,9},{2,18},{10... | collective-permute-start | bytes 294920 | tf_op jit(solution)/shard_map/ppermute | solution.py:331
  40.0 8.1 %collective-permute-start.14 = (bf16[384,256]{1,0:T(8,128)(2,1)}, bf16[384,256]{1,0:T(8,128)(2,1)S(1)}, u32[]{:S(2)}, u32[]{:S(2)}) collective-permute-start(bf16[384,256]{1,0:T(8,128)(2,1)} %get-tuple-element.30.refs_8_), channel_id=1, source_target_pairs={{0,16},{8,24},{16,0},{24,8},{1,17},{9,25},{17,1},{25,9},{2,18},{10... | collective-permute-start | bytes 589832 | tf_op jit(solution)/shard_map/ppermute | solution.py:331
  41.1 8.0 %collective-permute-start.12 = (bf16[384,256]{1,0:T(8,128)(2,1)}, bf16[384,256]{1,0:T(8,128)(2,1)S(1)}, u32[]{:S(2)}, u32[]{:S(2)}) collective-permute-start(bf16[384,256]{1,0:T(8,128)(2,1)} %get-tuple-element.30.refs_8_), channel_id=1, source_target_pairs={{0,8},{8,0},{16,24},{24,16},{1,9},{9,1},{17,25},{25,17},{2,10},{10... | collective-permute-start | bytes 589832 | tf_op jit(solution)/shard_map/ppermute | solution.py:331
  41.6 10.7 %collective-permute-start.15 = (bf16[384,256]{1,0:T(8,128)(2,1)}, bf16[384,256]{1,0:T(8,128)(2,1)S(1)}, u32[]{:S(2)}, u32[]{:S(2)}) collective-permute-start(bf16[384,256]{1,0:T(8,128)(2,1)} %get-tuple-element.31.refs_9_), channel_id=1, source_target_pairs={{0,16},{8,24},{16,0},{24,8},{1,17},{9,25},{17,1},{25,9},{2,18},{10... | collective-permute-start | bytes 589832 | tf_op jit(solution)/shard_map/ppermute | solution.py:331
  43.5 10.2 %collective-permute-start.19 = (bf16[384,256]{1,0:T(8,128)(2,1)}, bf16[384,256]{1,0:T(8,128)(2,1)S(1)}, u32[]{:S(2)}, u32[]{:S(2)}) collective-permute-start(bf16[384,256]{1,0:T(8,128)(2,1)} %get-tuple-element.31.refs_9_), channel_id=1, source_target_pairs={{0,1},{1,0},{2,3},{3,2},{4,5},{5,4},{6,7},{7,6},{8,9},{9,8},{10,11... | collective-permute-start | bytes 589832 | tf_op jit(solution)/shard_map/ppermute | solution.py:331
  43.5 10.2 %collective-permute-start.13 = (bf16[384,256]{1,0:T(8,128)(2,1)}, bf16[384,256]{1,0:T(8,128)(2,1)S(1)}, u32[]{:S(2)}, u32[]{:S(2)}) collective-permute-start(bf16[384,256]{1,0:T(8,128)(2,1)} %get-tuple-element.31.refs_9_), channel_id=1, source_target_pairs={{0,8},{8,0},{16,24},{24,16},{1,9},{9,1},{17,25},{25,17},{2,10},{10... | collective-permute-start | bytes 589832 | tf_op jit(solution)/shard_map/ppermute | solution.py:331
  48.0 6.2 %collective-permute-start.22 = (bf16[384,256]{1,0:T(8,128)(2,1)S(1)}, bf16[384,256]{1,0:T(8,128)(2,1)S(1)}, u32[]{:S(2)}, u32[]{:S(2)}) collective-permute-start(bf16[384,256]{1,0:T(8,128)(2,1)S(1)} %collective-permute-done.14.refs_12_), channel_id=1, source_target_pairs={{0,1},{1,0},{2,3},{3,2},{4,5},{5,4},{6,7},{7,6},{8,9},{9,8},{10,11... | collective-permute-start | bytes 589832 | tf_op jit(solution)/shard_map/ppermute | solution.py:331
  49.1 6.8 %collective-permute-start.16 = (bf16[384,256]{1,0:T(8,128)(2,1)S(1)}, bf16[384,256]{1,0:T(8,128)(2,1)S(1)}, u32[]{:S(2)}, u32[]{:S(2)}) collective-permute-start(bf16[384,256]{1,0:T(8,128)(2,1)S(1)} %collective-permute-done.12.refs_10_), channel_id=1, source_target_pairs={{0,16},{8,24},{16,0},{24,8},{1,17},{9,25},{17,1},{25,9},{2,18},{10... | collective-permute-start | bytes 589832 | tf_op jit(solution)/shard_map/ppermute | solution.py:331
  52.3 5.8 %collective-permute-start.17 = (bf16[384,256]{1,0:T(8,128)(2,1)S(1)}, bf16[384,256]{1,0:T(8,128)(2,1)S(1)}, u32[]{:S(2)}, u32[]{:S(2)}) collective-permute-start(bf16[384,256]{1,0:T(8,128)(2,1)S(1)} %collective-permute-done.15.refs_13_), channel_id=1, source_target_pairs={{0,8},{8,0},{16,24},{24,16},{1,9},{9,1},{17,25},{25,17},{2,10},{10... | collective-permute-start | bytes 589832 | tf_op jit(solution)/shard_map/ppermute | solution.py:331
  53.7 4.4 %collective-permute-start.20 = (bf16[384,256]{1,0:T(8,128)(2,1)S(1)}, bf16[384,256]{1,0:T(8,128)(2,1)S(1)}, u32[]{:S(2)}, u32[]{:S(2)}) collective-permute-start(bf16[384,256]{1,0:T(8,128)(2,1)S(1)} %collective-permute-done.12.refs_10_), channel_id=1, source_target_pairs={{0,1},{1,0},{2,3},{3,2},{4,5},{5,4},{6,7},{7,6},{8,9},{9,8},{10,11... | collective-permute-start | bytes 589832 | tf_op jit(solution)/shard_map/ppermute | solution.py:331
  71.1 11.0 %collective-permute-start.29 = (bf16[512,256]{1,0:T(8,128)(2,1)}, bf16[512,256]{1,0:T(8,128)(2,1)S(1)}, u32[]{:S(2)}, u32[]{:S(2)}) collective-permute-start(bf16[512,256]{1,0:T(8,128)(2,1)} %get-tuple-element.35), channel_id=1, source_target_pairs={{0,2},{6,4},{1,3},{7,5},{8,10},{14,12},{9,11},{15,13},{16,18},{22,... | collective-permute-start | bytes 786440 | tf_op jit(solution)/shard_map/ppermute | solution.py:377
  75.0 23.5 %collective-permute-start.28 = (bf16[512,256]{1,0:T(8,128)(2,1)}, bf16[512,256]{1,0:T(8,128)(2,1)S(1)}, u32[]{:S(2)}, u32[]{:S(2)}) collective-permute-start(bf16[512,256]{1,0:T(8,128)(2,1)} %get-tuple-element.33), channel_id=1, source_target_pairs={{0,4},{6,2},{1,5},{7,3},{8,12},{14,10},{9,13},{15,11},{16,20},{22,... | collective-permute-start | bytes 786440 | tf_op jit(solution)/shard_map/ppermute | solution.py:377
  78.5 20.1 %collective-permute-start.26 = (bf16[512,256]{1,0:T(8,128)(2,1)}, bf16[512,256]{1,0:T(8,128)(2,1)S(1)}, u32[]{:S(2)}, u32[]{:S(2)}) collective-permute-start(bf16[512,256]{1,0:T(8,128)(2,1)} %get-tuple-element.33), channel_id=1, source_target_pairs={{2,4},{4,2},{3,5},{5,3},{10,12},{12,10},{11,13},{13,11},{18,20},{2... | collective-permute-start | bytes 786440 | tf_op jit(solution)/shard_map/ppermute | solution.py:377
  79.2 19.4 %collective-permute-start.27 = (bf16[512,256]{1,0:T(8,128)(2,1)}, bf16[512,256]{1,0:T(8,128)(2,1)S(1)}, u32[]{:S(2)}, u32[]{:S(2)}) collective-permute-start(bf16[512,256]{1,0:T(8,128)(2,1)} %get-tuple-element.34), channel_id=1, source_target_pairs={{0,2},{2,0},{4,6},{6,4},{1,3},{3,1},{5,7},{7,5},{8,10},{10,8},{12,... | collective-permute-start | bytes 786440 | tf_op jit(solution)/shard_map/ppermute | solution.py:331
  83.0 15.6 %collective-permute-start.30 = (bf16[512,256]{1,0:T(8,128)(2,1)S(1)}, bf16[512,256]{1,0:T(8,128)(2,1)S(1)}, u32[]{:S(2)}, u32[]{:S(2)}) collective-permute-start(bf16[512,256]{1,0:T(8,128)(2,1)S(1)} %add_convert_fusion), channel_id=1, source_target_pairs={{2,6},{4,0},{3,7},{5,1},{10,14},{12,8},{11,15},{13,9},{18,22},{20,... | collective-permute-start | bytes 786440 | tf_op jit(solution)/shard_map/ppermute | solution.py:377
  84.3 8.8 %collective-permute-start.31 = (s32[32]{0:T(128)}, s32[32]{0:T(128)S(1)}, u32[]{:S(2)}, u32[]{:S(2)}) collective-permute-start(s32[32]{0:T(128)} %get-tuple-element.36), channel_id=1, source_target_pairs={{0,2},{2,0},{4,6},{6,4},{1,3},{3,1},{5,7},{7,5},{8,10},{10,8},{12,... | collective-permute-start | bytes 392 | tf_op jit(solution)/shard_map/ppermute | solution.py:331
  93.8 4.8 %collective-permute-start.32 = (s32[32]{0:T(128)S(1)}, s32[32]{0:T(128)S(1)}, u32[]{:S(2)}, u32[]{:S(2)}) collective-permute-start(s32[32]{0:T(128)S(1)} %add.19.refs_5_), channel_id=1, source_target_pairs={{0,4},{2,6},{4,0},{6,2},{1,5},{3,7},{5,1},{7,3},{8,12},{10,14},{12... | collective-permute-start | bytes 392 | tf_op jit(solution)/shard_map/ppermute | solution.py:331
  (38 other events, 116.7 us)
